TPU v7x, 128 devices: a whole 4x4x4 slice. The times are simulated.
128 devices in a mesh: rows: 32 (over x, z, core), cols: 4 (over y).
Axes of the slice: x: 4, y: 4, z: 4, core: 2. Of those that a mesh axis runs over, the one named last changes fastest.
Arguments:
- table: bfloat16 [262144, 512], P('rows', 'cols'), may hold values from -6 to 6
- item_ids: int32 [256, 256], P(('rows', 'cols')), may hold values from 0 to 262143, as said below
- cotangent: bfloat16 [256, 256, 512], P(('rows', 'cols')), may hold values from -6 to 6
- norm_gain: float32 [512], replicated, may hold values from 0.25 to 1.75
- w_in: bfloat16 [512, 2048], replicated, may hold values from -0.25 to 0.25
- bias_in: float32 [2048], replicated, may hold values from -3 to 3
- w_out: bfloat16 [2048, 512], replicated, may hold values from -0.125 to 0.125
Outputs:
- table_grad: float32 [262144, 512], P('rows', 'cols')
- w_in_grad: float32 [512, 2048], replicated
- bias_grad: float32 [2048], replicated
- w_out_grad: float32 [2048, 512], replicated
- gain_grad: float32 [512], replicated
Inputs may be any that keep to these rules, and one draw needn't show every extreme that they name: `item_ids`: within each device's 512 positions (aligned blocks of 2 sequences), at most 32 name rows of one range k * 8192 to (k + 1) * 8192 - 1; one range is named by exactly 32 positions of every device.
All inputs are finite; a program needn't handle non-finite values.
Results may differ from a plain program's by a relative error of at most 0.0051.
Values may be sent and summed in bfloat16 or wider, within the bound.
No kernel may reach another device: no remote copies, remote signals or barrier semaphores. Data moves between devices by JAX's collectives and lax.ppermute only.
A program may use at most 128 MiB of HBM per device.

v0:
```python
import math
import jax
import jax.numpy as jnp
from jax import lax
from jax.sharding import PartitionSpec as P

norm_eps = 1e-06
gelu_coef = 0.7978845608


def local_pass(embedded, d_out, norm_gain, w_in, bias_in, w_out):
    x_float = embedded.astype(jnp.float32)
    inv_rms = lax.rsqrt(jnp.mean(x_float * x_float, axis=-1, keepdims=True) + norm_eps)
    x_hat = x_float * inv_rms
    normed = (x_hat * norm_gain).astype(jnp.bfloat16)
    pre_act = jnp.dot(normed, w_in, preferred_element_type=jnp.float32) + bias_in
    tanh_part = jnp.tanh(gelu_coef * (pre_act + 0.044715 * pre_act * pre_act * pre_act))
    hidden = (0.5 * pre_act * (1.0 + tanh_part)).astype(jnp.bfloat16)
    d_act = lax.dot_general(
        d_out, w_out, (((1,), (1,)), ((), ())), preferred_element_type=jnp.float32
    )
    slope = 0.5 * (1.0 + tanh_part) + 0.5 * pre_act * (1.0 - tanh_part * tanh_part) * gelu_coef * (
        1.0 + 3.0 * 0.044715 * pre_act * pre_act
    )
    d_pre = d_act * slope
    d_pre_bf = d_pre.astype(jnp.bfloat16)
    g_out = lax.dot_general(
        hidden, d_out, (((0,), (0,)), ((), ())), preferred_element_type=jnp.float32
    )
    g_in = lax.dot_general(
        normed, d_pre_bf, (((0,), (0,)), ((), ())), preferred_element_type=jnp.float32
    )
    g_bias = jnp.sum(d_pre, axis=0)
    d_norm = lax.dot_general(
        d_pre_bf, w_in, (((1,), (1,)), ((), ())), preferred_element_type=jnp.float32
    )
    g_gain = jnp.sum(d_norm * x_hat, axis=0)
    scaled = d_norm * norm_gain
    d_embed = inv_rms * (
        scaled - x_hat * jnp.mean(scaled * x_hat, axis=-1, keepdims=True)
    ) + d_out.astype(jnp.float32)
    return (d_embed, g_in, g_bias, g_out, g_gain)


def local(table, item_ids, cotangent, norm_gain, w_in, bias_in, w_out):
    n_rows = lax.axis_size("rows")
    n_cols = lax.axis_size("cols")
    rows_dev = table.shape[0]
    col_width = table.shape[1]
    flat_ids = item_ids.reshape(-1)
    n_tokens = flat_ids.shape[0]
    capacity = max(2, 2 * n_tokens // n_rows)
    owners = flat_ids // rows_dev
    offsets = flat_ids - owners * rows_dev
    range_ids = jnp.arange(n_rows, dtype=jnp.int32)
    onehot = (owners[:, None] == range_ids[None, :]).astype(jnp.float32)
    tok_ids = jnp.arange(n_tokens, dtype=jnp.int32)
    lower = (tok_ids[:, None] >= tok_ids[None, :]).astype(jnp.float32)
    running = jnp.dot(lower, onehot, preferred_element_type=jnp.float32)
    rank_tok = (jnp.sum(running * onehot, axis=1) - 1.0).astype(jnp.int32)
    slot_of = owners * capacity + rank_tok
    n_slots = n_rows * capacity
    slot_ids = jnp.arange(n_slots, dtype=jnp.int32)
    slot_hit = slot_of[:, None] == slot_ids[None, :]
    wanted = jnp.sum(jnp.where(slot_hit, offsets[:, None], 0), axis=0).reshape(n_rows, capacity)
    requests = jnp.broadcast_to(wanted[:, None, :], (n_rows, n_cols, capacity)).reshape(
        n_rows * n_cols, capacity
    )
    looked = jnp.take(
        table,
        lax.all_to_all(requests, ("rows", "cols"), split_axis=0, concat_axis=0, tiled=True),
        axis=0,
    )
    fetched = lax.all_to_all(looked, ("rows", "cols"), split_axis=0, concat_axis=0, tiled=True)
    width = n_cols * col_width
    by_slot = jnp.transpose(
        fetched.reshape(n_rows, n_cols, capacity, col_width), (0, 2, 1, 3)
    ).reshape(n_slots, width)
    embedded = jnp.dot(
        slot_hit.astype(jnp.bfloat16), by_slot, preferred_element_type=jnp.float32
    ).astype(jnp.bfloat16)
    d_out = cotangent.reshape(n_tokens, width)
    block_rows = 512
    n_blocks = n_tokens // block_rows
    ff_width = w_in.shape[1]

    def one_block(carry, block):
        acc_in, acc_bias, acc_out, acc_gain = carry
        d_embed, g_in, g_bias, g_out, g_gain = local_pass(
            block[0], block[1], norm_gain, w_in, bias_in, w_out
        )
        return ((acc_in + g_in, acc_bias + g_bias, acc_out + g_out, acc_gain + g_gain), d_embed)

    start = (
        jnp.zeros((width, ff_width), jnp.float32),
        jnp.zeros((ff_width,), jnp.float32),
        jnp.zeros((ff_width, width), jnp.float32),
        jnp.zeros((width,), jnp.float32),
    )
    totals, d_blocks = lax.scan(
        one_block,
        start,
        (embedded.reshape(n_blocks, block_rows, width), d_out.reshape(n_blocks, block_rows, width)),
    )
    g_in, g_bias, g_out, g_gain = totals
    d_embed = d_blocks.reshape(n_tokens, width)
    slot_grad = lax.dot_general(
        slot_hit.astype(jnp.float32),
        d_embed,
        (((0,), (0,)), ((), ())),
        precision=lax.Precision.HIGHEST,
        preferred_element_type=jnp.float32,
    )
    payload = jnp.transpose(slot_grad.reshape(n_rows, capacity, n_cols, col_width), (0, 2, 1, 3))
    arrived, arrived_off = (
        lax.all_to_all(
            payload.reshape(n_rows * n_cols, capacity, col_width),
            ("rows", "cols"),
            split_axis=0,
            concat_axis=0,
            tiled=True,
        ),
        lax.all_to_all(requests, ("rows", "cols"), split_axis=0, concat_axis=0, tiled=True),
    )
    table_grad = (
        jnp.zeros((rows_dev, col_width), jnp.float32)
        .at[arrived_off.reshape(-1)]
        .add(arrived.reshape(-1, col_width))
    )
    summed = lax.psum((g_in, g_bias, g_out, g_gain), ("rows", "cols"))
    scale = 1.0 / math.sqrt(n_tokens * n_rows * n_cols)
    return (table_grad, summed[0] * scale, summed[1] * scale, summed[2] * scale, summed[3] * scale)


def solution(mesh):
    return jax.shard_map(
        local,
        mesh=mesh,
        in_specs=(
            P("rows", "cols"),
            P(("rows", "cols"), None),
            P(("rows", "cols"), None, None),
            P(),
            P(),
            P(),
            P(),
        ),
        out_specs=(P("rows", "cols"), P(), P(), P(), P()),
        check_vma=False,
    )
```

profile of v0, /device:TPU:1, one launch (start us, length us, event | category | flops | bytes accessed | tf_op | source)
XLA Modules:
  0.0 274.7 jit_solution(9714781316654998836)
XLA Ops:
  7.2 0.0 copy-start
  7.2 0.0 all-reduce.4.cloned.1.call-start
  7.2 0.8 copy.22
  8.1 0.3 fusion.18
  8.4 0.3 select_reduce_fusion
  8.6 0.1 broadcast_in_dim.60
  8.7 21.2 %all_to_all.26 = s32[128,1,32]{2,1,0:T(1,128)S(1)} all-to-all(s32[128,1,32]{2,1,0:T(1,128)S(1)} %bitcast.52), channel_id=1, replica_groups=mesh['rows'=32,'cols'=4] {'rows','cols'}, dimensions={0} | all-to-all | bytes 32768 | tf_op jit(solution)/shard_map/all_to_all | solution.py:123
  30.0 0.1 reshape.200
  30.1 12.9 %gather_fusion = bf16[4096,128]{1,0:T(8,128)(2,1)S(1)} fusion(bf16[8192,128]{1,0:T(8,128)(2,1)} %param.7, s32[4096]{0:T(1024)S(1)} %broadcast_clamp_fusion), kind=kCustom, calls=%fused_computation | custom fusion | bytes 2113536 | tf_op jit(solution)/shard_map/jit(_take)/gather | solution.py:69
  43.0 0.8 broadcast_select_fusion
  43.8 0.0 copy-start.4
  43.8 23.5 %all_to_all.27 = bf16[128,32,128]{2,1,0:T(8,128)(2,1)S(1)} all-to-all(bf16[128,32,128]{2,1,0:T(8,128)(2,1)S(1)} %broadcast_select_fusion), channel_id=1, replica_groups=mesh['rows'=32,'cols'=4] {'rows','cols'}, dimensions={0} | all-to-all | bytes 2097152 | tf_op jit(solution)/shard_map/all_to_all | solution.py:74
  67.3 0.5 copy.18
  67.8 0.9 fusion.25
  68.8 0.0 copy-start.3
  68.8 0.0 copy-start.6
  68.8 0.0 copy-done
  68.8 0.0 copy-done.4
  68.8 1.4 fusion.36
  70.2 0.0 copy-done.3
  70.2 0.0 copy-done.6
  70.2 0.0 copy-start.5
  70.2 4.2 %fusion.9 = f32[2048,512]{1,0:T(8,128)} fusion(bf16[512,512]{1,0:T(8,128)(2,1)S(1)} %bitcast.50, f32[512,2048]{1,0:T(8,128)S(1)} %fusion.36, f32[2048]{0:T(1024)S(1)} %copy-done.6), kind=kOutput, calls=%fused_computation.18 | convolution fusion | flops 1084227584 | bytes 8921088 | tf_op jit(solution)/shard_map/while/body/eval_jaxpr/dot_general | solution.py:27
  74.4 0.0 copy-done.5
  74.4 3.6 %fusion.45 = (f32[2048]{0:T(1024)S(1)}, bf16[512,2048]{1,0:T(8,128)(2,1)S(1)}) fusion(f32[512,2048]{1,0:T(8,128)S(1)} %fusion.36, f32[2048]{0:T(1024)S(1)} %copy-done.6, bf16[512,512]{1,0:T(8,128)(2,1)S(1)} %bitcast.51, bf16[2048,512]{1,0:T(8,128)(2,1)S(1)} %copy-done.5), kind=kOutput, calls=%fused_computation.75 | convolution fusion | flops 1095759872 | bytes 8929280 | tf_op jit(solution)/shard_map/while/body/eval_jaxpr/dot_general | solution.py:19
  78.0 0.0 copy-start.2
  78.0 1.3 copy-done.2
  79.3 3.3 %fusion.28 = f32[512,2048]{1,0:T(8,128)} fusion(bf16[512,2048]{1,0:T(8,128)(2,1)S(1)} %get-tuple-element.53, bf16[512,512]{0,1:T(8,128)(2,1)S(1)} %get-tuple-element.50, f32[512]{0:T(512)S(1)} %copy-done.4, f32[512]{0:T(512)S(1)} %add_rsqrt_fusion), kind=kOutput, calls=%fused_computation.40 | convolution fusion | flops 1074790400 | bytes 6819840 | tf_op jit(solution)/shard_map/while/body/eval_jaxpr/dot_general | solution.py:30
  82.6 0.0 all-reduce.4.cloned.1.call-update
  82.7 1.3 copy.21
  83.9 3.0 %fusion.24 = (f32[512]{0:T(512)S(1)}, f32[512]{0:T(512)S(1)}, f32[512,512]{0,1:T(8,128)S(1)}) fusion(bf16[512,512]{0,1:T(8,128)(2,1)S(1)} %get-tuple-element.50, f32[512]{0:T(512)S(1)} %add_rsqrt_fusion, f32[512]{0:T(512)S(1)} %copy-done.4, bf16[512,2048]{1,0:T(8,128)(2,1)S(1)} %copy-done, bf16[512,2048]{1,0:T(8,128)(2,1)} %copy-done.2), kind=kOutput, calls=%fused_computation.36 | convolution fusion | flops 1075575808 | bytes 5775360 | tf_op jit(solution)/shard_map/while/body/eval_jaxpr/dot_general | solution.py:34
  87.0 0.3 fusion.23
  87.3 3.2 %fusion.10 = f32[32,32,4,128]{3,1,2,0:T(8,128)} fusion(f32[4,128,512,1]{2,1,0,3:T(8,128)S(1)} %bitcast.45, s32[32,32]{1,0:T(8,128)S(1)} %multiply_add_fusion.1, s32[512]{0:T(512)S(1)} %convert_add_fusion), kind=kOutput, calls=%fused_computation.19 | convolution fusion | flops 3221749760 | bytes 3151872 | tf_op jit(solution)/shard_map/dot_general | solution.py:107
  90.5 4.8 %all-to-all-start.2 = ((f32[128,32,128]{2,1,0:T(8,128)}), f32[128,32,128]{2,1,0:T(8,128)}, u32[]{:S(2)}, u32[]{:S(2)}) async-start(f32[128,32,128]{2,1,0:T(8,128)} %bitcast.42), calls=%async_computation.2 | async-start | bytes 4194304 | tf_op jit(solution)/shard_map/all_to_all | solution.py:116
  95.3 0.5 broadcast.230
  95.8 0.8 reduce.3
  96.7 0.1 reshape.193
  96.8 85.3 %all-reduce = (f32[2048]{0:T(1024)S(1)}, f32[512]{0:T(512)S(1)}) all-reduce(f32[2048]{0:T(1024)S(1)} %get-tuple-element.52, f32[512]{0:T(512)S(1)} %get-tuple-element.29), channel_id=1, replica_groups=mesh['rows'=32,'cols'=4] {'rows','cols'}, use_global_device_ids=true, to_apply=%region_7.8 | all-reduce | flops 2560 | bytes 20480 | tf_op jit(solution)/shard_map/psum | solution.py:130
  182.1 0.6 broadcast_multiply_fusion.3
  182.7 0.6 broadcast_multiply_fusion.2
  183.3 0.0 all-to-all-done.2
  183.3 25.4 %scatter_custom_fusion = f32[8192,128]{1,0:T(8,128)} fusion(s32[4096]{0:T(1024)S(1)} %bitcast.53, f32[4096,128]{1,0:T(8,128)} %bitcast.15, f32[]{:T(128)} %constant.40.clone.1), kind=kCustom, calls=%fused_computation.16 | custom fusion | flops 524288 | bytes 4194816 | tf_op jit(solution)/shard_map/scatter-add | solution.py:128
  208.7 51.7 %all-reduce.4.cloned.1.call-done = (f32[512,2048]{1,0:T(8,128)}, f32[2048,512]{1,0:T(8,128)}) async-done(((f32[512,2048]{1,0:T(8,128)}, f32[2048,512]{1,0:T(8,128)}), (f32[512,2048]{1,0:T(8,128)}, f32[2048,512]{1,0:T(8,128)})) %all-reduce.4.cloned.1.call-update) | async-done | bytes 8388624 | tf_op jit(solution)/shard_map/psum | solution.py:130
  260.4 0.0 copy-start.1
  260.4 4.9 %broadcast_multiply_fusion.1 = f32[512,2048]{1,0:T(8,128)} fusion(f32[512,2048]{1,0:T(8,128)} %get-tuple-element.33), kind=kLoop, calls=%fused_computation.12 | loop fusion | flops 1048576 | bytes 8388608 | tf_op jit(solution)/shard_map/mul | solution.py:132
  265.3 0.0 copy-done.1
  265.3 2.5 broadcast_multiply_fusion
  (10 shorter events, 0.1 us)
Async XLA Ops:
  7.2 61.6 %copy-start = (bf16[512,2048]{1,0:T(8,128)(2,1)S(1)}, bf16[512,2048]{1,0:T(8,128)(2,1)}, u32[]{:S(2)}) copy-start(bf16[512,2048]{1,0:T(8,128)(2,1)} %param.11) | copy-start | bytes 6291460
  7.2 253.2 %all-reduce.4.cloned.1.call-start = ((), (), s32[]{:S(2)}) async-start(), calls=%async_computation.3 | async-start | bytes 16777216 | tf_op jit(solution)/shard_map/psum | solution.py:130
  43.8 25.0 %copy-start.4 = (f32[512]{0:T(512)S(1)}, f32[512]{0:T(512)}, u32[]{:S(2)}) copy-start(f32[512]{0:T(512)} %param.10) | copy-start | bytes 6148
  68.8 1.4 copy-start.3
  68.8 1.4 copy-start.6
  70.2 4.2 %copy-start.5 = (bf16[2048,512]{1,0:T(8,128)(2,1)S(1)}, bf16[2048,512]{1,0:T(8,128)(2,1)}, u32[]{:S(2)}) copy-start(bf16[2048,512]{1,0:T(8,128)(2,1)} %param.13) | copy-start | bytes 6291460
  78.0 1.3 copy-start.2
  90.5 92.8 %all-to-all-start.2 = ((f32[128,32,128]{2,1,0:T(8,128)}), f32[128,32,128]{2,1,0:T(8,128)}, u32[]{:S(2)}, u32[]{:S(2)}) async-start(f32[128,32,128]{2,1,0:T(8,128)} %bitcast.42), calls=%async_computation.2 | async-start | bytes 4194304 | tf_op jit(solution)/shard_map/all_to_all | solution.py:116
  260.4 4.9 %copy-start.1 = (f32[2048,512]{1,0:T(8,128)S(1)}, f32[2048,512]{1,0:T(8,128)}, u32[]{:S(2)}) copy-start(f32[2048,512]{1,0:T(8,128)} %get-tuple-element.34) | copy-start | bytes 12582916
Sparse Core Ops, SparseCore 0:
  82.8 177.5 all-reduce.3
where the time goes:
time: 275 us
  blocking collectives  130 us (47%)
  waiting for transfers between devices  51.7 us (19%)
  other arithmetic  36.3 us (13%)
  matrix products  19.9 us (7%)
  local copies, waits for them, and re-layouts  17.6 us (6%)
  between operations  14.2 us (5%)
  starting transfers between devices  4.84 us (2%)
    psum x1, blocking collectives, local(): summed = lax.psum((g_in, g_bias, g_out, g_gain), ('rows', 'cols'))  85.3 us
    psum x1, waiting for transfers between devices, local(): summed = lax.psum((g_in, g_bias, g_out, g_gain), ('rows', 'cols'))  51.7 us
    scatter-add x1, other arithmetic, local(): table_grad = jnp.zeros((rows_dev, col_width), jnp.float32).at[arrived_off...  25.4 us
    all_to_all x1, blocking collectives, local(): lax.all_to_all(looked, ('rows', 'cols'), split_axis=0, concat_axis=0, til...  23.5 us
    all_to_all x1, blocking collectives, local(): lax.all_to_all(requests, ('rows', 'cols'), split_axis=0, concat_axis=0, t...  21.2 us
    gather x1, local copies, waits for them, and re-layouts, local(): jnp.take(table, lax.all_to_all(requests, ('rows', 'cols'), split_axis=0,...  12.9 us
  transfers between devices with their start and end apart: 2, of which 1 were waited for; matrix products, arithmetic and copies ran while one was open for 13% of the time, Pallas kernels for 0%

commit v1 on v0

--- a/solution.py
+++ b/solution.py
@@ -127,7 +127,9 @@
         .at[arrived_off.reshape(-1)]
         .add(arrived.reshape(-1, col_width))
     )
-    summed = lax.psum((g_in, g_bias, g_out, g_gain), ("rows", "cols"))
+    summed = (g_in, g_bias, g_out, g_gain)
+    for mesh_axis in ("rows", "cols"):
+        summed = lax.psum(summed, mesh_axis)
     scale = 1.0 / math.sqrt(n_tokens * n_rows * n_cols)
     return (table_grad, summed[0] * scale, summed[1] * scale, summed[2] * scale, summed[3] * scale)
 

time: 275 us -> 416 us (1.51); the launches traced: 275 us -> 409 us
  blocking collectives: 130 us -> 197 us
  waiting for transfers between devices: 51.7 us -> 116 us
    psum x1 -> x2, blocking collectives: 85.3 us -> 152 us  [local(): summed = lax.psum(summed, mesh_axis)]
    psum x1 -> x2, waiting for transfers between devices: 51.7 us -> 116 us  [local(): summed = lax.psum(summed, mesh_axis)]
  transfers between devices with their start and end apart: 2 -> 3, of which waited for: 1 -> 1; matrix products, arithmetic and copies ran while one was open for 13% -> 9% of each run, Pallas kernels for 0% -> 0%
where the time goes in v1:
time: 416 us; the launch traced here: 409 us
  blocking collectives  197 us (47%)
  waiting for transfers between devices  116 us (28%)
  other arithmetic  36.1 us (9%)
  matrix products  19.9 us (5%)
  local copies, waits for them, and re-layouts  17.6 us (4%)
  between operations  14.3 us (3%)
  starting transfers between devices  8.65 us (2%)
    psum x2, blocking collectives, local(): summed = lax.psum(summed, mesh_axis)  152 us
    psum x2, waiting for transfers between devices, local(): summed = lax.psum(summed, mesh_axis)  116 us
    scatter-add x1, other arithmetic, local(): table_grad = jnp.zeros((rows_dev, col_width), jnp.float32).at[arrived_off...  25.4 us
    all_to_all x1, blocking collectives, local(): lax.all_to_all(looked, ('rows', 'cols'), split_axis=0, concat_axis=0, til...  23.5 us
    all_to_all x1, blocking collectives, local(): lax.all_to_all(requests, ('rows', 'cols'), split_axis=0, concat_axis=0, t...  21.2 us
    gather x1, local copies, waits for them, and re-layouts, local(): jnp.take(table, lax.all_to_all(requests, ('rows', 'cols'), split_axis=0,...  12.9 us
    all_to_all x1, starting transfers between devices, local(): lax.all_to_all(payload.reshape(n_rows * n_cols, capacity, col_width), ('r...  8.39 us
  transfers between devices with their start and end apart: 3, of which 1 were waited for; matrix products, arithmetic and copies ran while one was open for 9% of the time, Pallas kernels for 0%

profile of v1, /device:TPU:1, one launch (start us, length us, event | category | flops | bytes accessed | tf_op | source)
XLA Modules:
  0.0 409.1 jit_solution(12482663006456205413)
XLA Ops:
  7.2 0.0 copy-start
  7.2 0.0 all-reduce.7.cloned.1.call-start
  7.2 0.8 copy.22
  8.1 0.3 fusion.18
  8.4 0.3 select_reduce_fusion
  8.6 0.1 broadcast_in_dim.60
  8.7 21.2 %all_to_all.26 = s32[128,1,32]{2,1,0:T(1,128)S(1)} all-to-all(s32[128,1,32]{2,1,0:T(1,128)S(1)} %bitcast.52), channel_id=1, replica_groups=mesh['rows'=32,'cols'=4] {'rows','cols'}, dimensions={0} | all-to-all | bytes 32768 | tf_op jit(solution)/shard_map/all_to_all | solution.py:123
  29.9 0.1 reshape.200
  30.1 12.9 %gather_fusion = bf16[4096,128]{1,0:T(8,128)(2,1)S(1)} fusion(bf16[8192,128]{1,0:T(8,128)(2,1)} %param.7, s32[4096]{0:T(1024)S(1)} %broadcast_clamp_fusion), kind=kCustom, calls=%fused_computation | custom fusion | bytes 2113536 | tf_op jit(solution)/shard_map/jit(_take)/gather | solution.py:69
  43.0 0.8 broadcast_select_fusion
  43.8 0.0 copy-start.4
  43.8 23.5 %all_to_all.27 = bf16[128,32,128]{2,1,0:T(8,128)(2,1)S(1)} all-to-all(bf16[128,32,128]{2,1,0:T(8,128)(2,1)S(1)} %broadcast_select_fusion), channel_id=1, replica_groups=mesh['rows'=32,'cols'=4] {'rows','cols'}, dimensions={0} | all-to-all | bytes 2097152 | tf_op jit(solution)/shard_map/all_to_all | solution.py:74
  67.3 0.5 copy.18
  67.8 0.9 fusion.25
  68.8 0.0 copy-start.3
  68.8 0.0 copy-start.6
  68.8 0.0 copy-done
  68.8 0.0 copy-done.4
  68.8 1.4 fusion.36
  70.2 0.0 copy-done.3
  70.2 0.0 copy-done.6
  70.2 0.0 copy-start.5
  70.2 4.2 %fusion.9 = f32[2048,512]{1,0:T(8,128)} fusion(bf16[512,512]{1,0:T(8,128)(2,1)S(1)} %bitcast.50, f32[512,2048]{1,0:T(8,128)S(1)} %fusion.36, f32[2048]{0:T(1024)S(1)} %copy-done.6), kind=kOutput, calls=%fused_computation.18 | convolution fusion | flops 1084227584 | bytes 8921088 | tf_op jit(solution)/shard_map/while/body/eval_jaxpr/dot_general | solution.py:27
  74.4 0.0 copy-done.5
  74.4 3.6 fusion.45
  78.0 0.0 copy-start.2
  78.0 1.3 copy-done.2
  79.3 3.3 fusion.28
  82.6 0.0 all-reduce.7.cloned.1.call-update
  82.7 0.2 all-reduce.9.cloned.1.call-start
  82.9 116.0 %all-reduce.7.cloned.1.call-done = (f32[512,2048]{1,0:T(8,128)}, f32[2048,512]{1,0:T(8,128)}) async-done(((f32[512,2048]{1,0:T(8,128)}, f32[2048,512]{1,0:T(8,128)}), (f32[512,2048]{1,0:T(8,128)}, f32[2048,512]{1,0:T(8,128)})) %all-reduce.7.cloned.1.call-update) | async-done | bytes 8388624 | tf_op jit(solution)/shard_map/psum | solution.py:132
  198.8 0.0 all-reduce.9.cloned.1.call-update
  198.9 1.3 copy.21
  200.1 3.0 fusion.24
  203.2 0.3 fusion.23
  203.5 3.2 fusion.10
  206.7 8.4 %all-to-all-start.2 = ((f32[128,32,128]{2,1,0:T(8,128)}), f32[128,32,128]{2,1,0:T(8,128)}, u32[]{:S(2)}, u32[]{:S(2)}) async-start(f32[128,32,128]{2,1,0:T(8,128)} %bitcast.42), calls=%async_computation.2 | async-start | bytes 4194304 | tf_op jit(solution)/shard_map/all_to_all | solution.py:116
  215.1 0.5 broadcast.230
  215.7 0.8 reduce.3
  216.5 0.1 reshape.193
  216.6 138.0 %all-reduce = (f32[2048]{0:T(1024)S(1)}, f32[512]{0:T(512)S(1)}) all-reduce(f32[2048]{0:T(1024)S(1)} %get-tuple-element.56, f32[512]{0:T(512)S(1)} %get-tuple-element.29), channel_id=1, replica_groups=mesh['rows'=32,'cols'=4] {'rows'}, use_global_device_ids=true, to_apply=%region_8.9 | all-reduce | flops 2560 | bytes 20480 | tf_op jit(solution)/shard_map/psum | solution.py:132
  354.6 13.9 %all-reduce.2 = (f32[2048]{0:T(1024)S(1)}, f32[512]{0:T(512)S(1)}) all-reduce(f32[2048]{0:T(1024)S(1)} %get-tuple-element.31, f32[512]{0:T(512)S(1)} %get-tuple-element.32), channel_id=1, replica_groups=mesh['rows'=32,'cols'=4] {'cols'}, use_global_device_ids=true, to_apply=%region_9.10 | all-reduce | flops 2560 | bytes 20480 | tf_op jit(solution)/shard_map/psum | solution.py:132
  368.5 0.6 broadcast_multiply_fusion.3
  369.0 0.6 broadcast_multiply_fusion.2
  369.6 0.0 all-to-all-done.2
  369.6 25.4 %scatter_custom_fusion = f32[8192,128]{1,0:T(8,128)} fusion(s32[4096]{0:T(1024)S(1)} %bitcast.53, f32[4096,128]{1,0:T(8,128)} %bitcast.15, f32[]{:T(128)} %constant.40.clone.1), kind=kCustom, calls=%fused_computation.16 | custom fusion | flops 524288 | bytes 4194816 | tf_op jit(solution)/shard_map/scatter-add | solution.py:128
  395.0 4.9 %broadcast_multiply_fusion = f32[2048,512]{1,0:T(8,128)} fusion(f32[2048,512]{1,0:T(8,128)} %get-tuple-element.50), kind=kLoop, calls=%fused_computation.11 | loop fusion | flops 1048576 | bytes 8388608 | tf_op jit(solution)/shard_map/mul | solution.py:134
  399.9 2.3 broadcast_multiply_fusion.1
  (13 shorter events, 0.1 us)
Async XLA Ops:
  7.2 61.6 %copy-start = (bf16[512,2048]{1,0:T(8,128)(2,1)S(1)}, bf16[512,2048]{1,0:T(8,128)(2,1)}, u32[]{:S(2)}) copy-start(bf16[512,2048]{1,0:T(8,128)(2,1)} %param.11) | copy-start | bytes 6291460
  7.2 191.7 %all-reduce.7.cloned.1.call-start = ((), (), s32[]{:S(2)}) async-start(), calls=%async_computation.3 | async-start | bytes 16777216 | tf_op jit(solution)/shard_map/psum | solution.py:132
  43.8 25.0 %copy-start.4 = (f32[512]{0:T(512)S(1)}, f32[512]{0:T(512)}, u32[]{:S(2)}) copy-start(f32[512]{0:T(512)} %param.10) | copy-start | bytes 6148
  68.8 1.4 copy-start.3
  68.8 1.4 copy-start.6
  70.2 4.2 %copy-start.5 = (bf16[2048,512]{1,0:T(8,128)(2,1)S(1)}, bf16[2048,512]{1,0:T(8,128)(2,1)}, u32[]{:S(2)}) copy-start(bf16[2048,512]{1,0:T(8,128)(2,1)} %param.13) | copy-start | bytes 6291460
  78.0 1.3 copy-start.2
  82.7 312.4 %all-reduce.9.cloned.1.call-start = ((), (), s32[]{:S(2)}) async-start(), calls=%async_computation.4 | async-start | bytes 16777216 | tf_op jit(solution)/shard_map/psum | solution.py:132
  206.7 162.9 %all-to-all-start.2 = ((f32[128,32,128]{2,1,0:T(8,128)}), f32[128,32,128]{2,1,0:T(8,128)}, u32[]{:S(2)}, u32[]{:S(2)}) async-start(f32[128,32,128]{2,1,0:T(8,128)} %bitcast.42), calls=%async_computation.2 | async-start | bytes 4194304 | tf_op jit(solution)/shard_map/all_to_all | solution.py:116
  395.0 4.9 %copy-start.1 = (f32[512,2048]{1,0:T(8,128)S(1)}, f32[512,2048]{1,0:T(8,128)}, u32[]{:S(2)}) copy-start(f32[512,2048]{1,0:T(8,128)} %get-tuple-element.49) | copy-start | bytes 12582916
Sparse Core Ops, SparseCore 0:
  82.8 116.0 all-reduce.6
  201.6 183.0 all-reduce.8
